TPU v7x, 512 devices: a whole 4x4x16 slice. The times are simulated.
512 devices in a mesh: row: 32 (over y, x, core), col: 16 (over z).
Axes of the slice: x: 4, y: 4, z: 16, core: 2. Of those that a mesh axis runs over, the one named last changes fastest.
Arguments:
- noise: bfloat16 [16384, 128], P('row'), may hold values from -6 to 6
- w_first: bfloat16 [128, 512], replicated, may hold values from -0.5 to 0.5
- w_second: bfloat16 [512, 1024], replicated, may hold values from -0.25 to 0.25
- history: bfloat16 [16384, 1024], P('col'), may hold values from -4 to 4
Outputs:
- grad_first: float32 [128, 512], replicated
- grad_second: float32 [512, 1024], P(None, 'col')
All inputs are finite; a program needn't handle non-finite values.
Results may differ from a plain program's by a relative error of at most 0.00085.
Values sent between devices are 32-bit elements; how exact they have to be, the bound alone decides.
A program may use at most 64 MiB of HBM per device.

v0:
```python
import math
import jax
import jax.numpy as jnp
from jax import lax
from jax.sharding import PartitionSpec as P

SWEEPS = 3
EPSILON = 0.01


def row_lse(scores):
    maxima = lax.pmax(jnp.max(scores, axis=1), "col")
    totals = lax.psum(jnp.sum(jnp.exp(scores - maxima[:, None]), axis=1), "col")
    return maxima + jnp.log(totals)


def col_lse(scores):
    maxima = lax.pmax(jnp.max(scores, axis=0), "row")
    totals = lax.psum(jnp.sum(jnp.exp(scores - maxima[None, :]), axis=0), "row")
    return maxima + jnp.log(totals)


def shards(noise, w_first, w_second, history):
    gen_total = noise.shape[0] * lax.axis_size("row")
    hist_total = history.shape[0] * lax.axis_size("col")
    width = w_second.shape[1]
    slice_width = width // lax.axis_size("col")
    col_start = lax.axis_index("col") * slice_width
    preact = jnp.dot(noise, w_first, preferred_element_type=jnp.float32)
    hidden = jax.nn.silu(preact).astype(jnp.bfloat16)
    surface = jnp.dot(hidden, w_second, preferred_element_type=jnp.float32).astype(jnp.bfloat16)
    surf_f = surface.astype(jnp.float32)
    hist_f = history.astype(jnp.float32)
    surf_sq = jnp.sum(surf_f * surf_f, axis=1)
    hist_sq = jnp.sum(hist_f * hist_f, axis=1)
    inner = lax.dot_general(
        surface, history, (((1,), (1,)), ((), ())), preferred_element_type=jnp.float32
    )
    cost_tile = (surf_sq[:, None] + hist_sq[None, :] - 2.0 * inner) / width
    f_pot = jnp.zeros((noise.shape[0],), jnp.float32)
    g_pot = jnp.zeros((history.shape[0],), jnp.float32)
    for sweep_no in range(SWEEPS):
        g_pot = -EPSILON * (-math.log(gen_total) + col_lse((f_pot[:, None] - cost_tile) / EPSILON))
        f_pot = -EPSILON * (-math.log(hist_total) + row_lse((g_pot[None, :] - cost_tile) / EPSILON))
    weights = (
        jnp.exp((f_pot[:, None] + g_pot[None, :] - cost_tile) / EPSILON) / hist_total
    ).astype(jnp.bfloat16)
    partial_value = jnp.dot(weights, history, preferred_element_type=jnp.float32)
    scale = 1.0 / math.sqrt(gen_total)
    barycentre = lax.psum(partial_value, "col")
    d_surface = ((surf_f - barycentre) * scale).astype(jnp.bfloat16)
    d_hidden = lax.dot_general(
        d_surface, w_second, (((1,), (1,)), ((), ())), preferred_element_type=jnp.float32
    )
    d_slice = lax.dynamic_slice_in_dim(d_surface, col_start, slice_width, 1)
    sigma = jax.nn.sigmoid(preact)
    d_preact = (d_hidden * sigma * (1.0 + preact * (1.0 - sigma))).astype(jnp.bfloat16)
    first_term = lax.dot_general(
        noise, d_preact, (((0,), (0,)), ((), ())), preferred_element_type=jnp.float32
    )
    second_term = lax.dot_general(
        hidden, d_slice, (((0,), (0,)), ((), ())), preferred_element_type=jnp.float32
    )
    grad_first, grad_second = lax.psum((first_term, second_term), "row")
    return (grad_first, grad_second)


def solution(mesh):
    placed = (P("row", None), P(), P(), P("col", None))
    return jax.shard_map(
        shards, mesh=mesh, in_specs=placed, out_specs=(P(), P(None, "col")), check_vma=False
    )
```

profile of v0, /device:TPU:1, one launch (start us, length us, event | category | flops | bytes accessed | tf_op | source)
XLA Modules:
  0.0 862.4 jit_solution(6891692069466334634)
XLA Ops:
  7.2 0.0 copy-start
  7.2 0.0 copy-start.7
  7.2 0.0 copy-start.6
  7.2 0.0 all-reduce.4.cloned.1.call-start
  7.2 2.2 multiply_reduce_fusion
  9.4 0.0 copy-done.7
  9.4 0.0 copy-done.6
  9.4 1.3 multiply_convert_fusion.2
  10.8 0.0 copy-done
  10.8 0.8 fusion
  11.6 0.0 copy-done.4
  11.6 1.0 copy-done.1
  12.5 1.5 fusion.3
  14.1 68.9 %pmax.42 = f32[1024]{0:T(1024)S(1)} all-reduce(f32[1024]{0:T(1024)S(1)} %get-tuple-element.10), channel_id=1, replica_groups=mesh['row'=32,'col'=16] {'row'}, use_global_device_ids=true, to_apply=%region_3.4 | all-reduce | flops 1024 | bytes 8192 | tf_op jit(solution)/shard_map/pmax | solution.py:18
  83.0 0.4 exponential_reduce_fusion.5
  83.4 62.7 %psum.63 = f32[1024]{0:T(1024)S(1)} all-reduce(f32[1024]{0:T(1024)S(1)} %exponential_reduce_fusion.5), channel_id=1, replica_groups=mesh['row'=32,'col'=16] {'row'}, use_global_device_ids=true, to_apply=%region_5.6 | all-reduce | flops 1024 | bytes 8192 | tf_op jit(solution)/shard_map/psum | solution.py:19
  146.1 0.3 fusion.4
  146.4 28.8 %pmax.43 = f32[512]{0:T(512)S(1)} all-reduce(f32[512]{0:T(512)S(1)} %fusion.4), channel_id=1, replica_groups=mesh['row'=32,'col'=16] {'col'}, use_global_device_ids=true, to_apply=%region_7.8 | all-reduce | flops 512 | bytes 4096 | tf_op jit(solution)/shard_map/pmax | solution.py:12
  175.2 0.6 exponential_reduce_fusion.4
  175.7 20.1 %psum.64 = f32[512]{0:T(512)S(1)} all-reduce(f32[512]{0:T(512)S(1)} %exponential_reduce_fusion.4), channel_id=1, replica_groups=mesh['row'=32,'col'=16] {'col'}, use_global_device_ids=true, to_apply=%region_9.10 | all-reduce | flops 512 | bytes 4096 | tf_op jit(solution)/shard_map/psum | solution.py:13
  195.8 0.3 fusion.5
  196.1 76.7 %pmax.44 = f32[1024]{0:T(1024)S(1)} all-reduce(f32[1024]{0:T(1024)S(1)} %fusion.5), channel_id=1, replica_groups=mesh['row'=32,'col'=16] {'row'}, use_global_device_ids=true, to_apply=%region_11.12 | all-reduce | flops 1024 | bytes 8192 | tf_op jit(solution)/shard_map/pmax | solution.py:18
  272.8 0.5 exponential_reduce_fusion.3
  273.3 62.7 %psum.65 = f32[1024]{0:T(1024)S(1)} all-reduce(f32[1024]{0:T(1024)S(1)} %exponential_reduce_fusion.3), channel_id=1, replica_groups=mesh['row'=32,'col'=16] {'row'}, use_global_device_ids=true, to_apply=%region_13.14 | all-reduce | flops 1024 | bytes 8192 | tf_op jit(solution)/shard_map/psum | solution.py:19
  335.9 0.3 fusion.6
  336.2 22.0 %pmax.45 = f32[512]{0:T(512)S(1)} all-reduce(f32[512]{0:T(512)S(1)} %fusion.6), channel_id=1, replica_groups=mesh['row'=32,'col'=16] {'col'}, use_global_device_ids=true, to_apply=%region_15.16 | all-reduce | flops 512 | bytes 4096 | tf_op jit(solution)/shard_map/pmax | solution.py:12
  358.2 0.6 exponential_reduce_fusion.2
  358.8 20.1 %psum.66 = f32[512]{0:T(512)S(1)} all-reduce(f32[512]{0:T(512)S(1)} %exponential_reduce_fusion.2), channel_id=1, replica_groups=mesh['row'=32,'col'=16] {'col'}, use_global_device_ids=true, to_apply=%region_17.18 | all-reduce | flops 512 | bytes 4096 | tf_op jit(solution)/shard_map/psum | solution.py:13
  378.9 0.3 fusion.7
  379.2 76.7 %pmax.46 = f32[1024]{0:T(1024)S(1)} all-reduce(f32[1024]{0:T(1024)S(1)} %fusion.7), channel_id=1, replica_groups=mesh['row'=32,'col'=16] {'row'}, use_global_device_ids=true, to_apply=%region_19.20 | all-reduce | flops 1024 | bytes 8192 | tf_op jit(solution)/shard_map/pmax | solution.py:18
  455.8 0.5 exponential_reduce_fusion.1
  456.3 62.7 %psum.67 = f32[1024]{0:T(1024)S(1)} all-reduce(f32[1024]{0:T(1024)S(1)} %exponential_reduce_fusion.1), channel_id=1, replica_groups=mesh['row'=32,'col'=16] {'row'}, use_global_device_ids=true, to_apply=%region_21.22 | all-reduce | flops 1024 | bytes 8192 | tf_op jit(solution)/shard_map/psum | solution.py:19
  519.0 0.3 fusion.8
  519.3 22.0 %pmax.47 = f32[512]{0:T(512)S(1)} all-reduce(f32[512]{0:T(512)S(1)} %fusion.8), channel_id=1, replica_groups=mesh['row'=32,'col'=16] {'col'}, use_global_device_ids=true, to_apply=%region_23.24 | all-reduce | flops 512 | bytes 4096 | tf_op jit(solution)/shard_map/pmax | solution.py:12
  541.3 0.6 exponential_reduce_fusion
  541.9 20.1 %psum.68 = f32[512]{0:T(512)S(1)} all-reduce(f32[512]{0:T(512)S(1)} %exponential_reduce_fusion), channel_id=1, replica_groups=mesh['row'=32,'col'=16] {'col'}, use_global_device_ids=true, to_apply=%region_25.26 | all-reduce | flops 512 | bytes 4096 | tf_op jit(solution)/shard_map/psum | solution.py:13
  562.0 4.2 fusion.13
  566.2 0.0 all-reduce.4.cloned.1.call-update
  566.2 0.0 all-reduce.6.cloned.1.call-start
  566.2 141.2 %all-reduce.4.cloned.1.call-done = f32[512,1024]{1,0:T(8,128)} async-done(((f32[512,1024]{1,0:T(8,128)}), f32[512,1024]{1,0:T(8,128)}) %all-reduce.4.cloned.1.call-update) | async-done | bytes 2097168 | tf_op jit(solution)/shard_map/psum | solution.py:50
  707.5 0.0 copy-done.3
  707.5 2.0 fusion.2
  709.5 1.0 fusion.22
  710.5 3.1 fusion.12
  713.6 0.0 all-reduce.6.cloned.1.call-update
  713.6 138.6 %all-reduce.6.cloned.1.call-done = (f32[128,512]{0,1:T(8,128)}, f32[512,64]{0,1:T(8,128)}) async-done(((f32[128,512]{0,1:T(8,128)}, f32[512,64]{0,1:T(8,128)}), (f32[128,512]{0,1:T(8,128)}, f32[512,64]{0,1:T(8,128)})) %all-reduce.6.cloned.1.call-update) | async-done | bytes 393232 | tf_op jit(solution)/shard_map/psum | solution.py:64
  852.2 1.8 copy.6
  854.0 1.6 copy.10
  (13 shorter events, 0.1 us)
Async XLA Ops:
  7.2 3.6 copy-start
  7.2 2.2 copy-start.7
  7.2 2.2 copy-start.6
  7.2 700.3 %all-reduce.4.cloned.1.call-start = ((), (), s32[]{:S(2)}) async-start(), calls=%async_computation | async-start | bytes 4194304 | tf_op jit(solution)/shard_map/psum | solution.py:50
  10.8 0.8 copy-start.4
  10.8 1.8 copy-start.1
  11.6 2.5 copy-start.2
  566.2 141.3 %copy-start.3 = (bf16[512,1024]{1,0:T(8,128)(2,1)S(1)}, bf16[512,1024]{1,0:T(8,128)(2,1)}, u32[]{:S(2)}) copy-start(bf16[512,1024]{1,0:T(8,128)(2,1)} %copy-done.2) | copy-start | bytes 3145732
  566.2 286.0 %all-reduce.6.cloned.1.call-start = ((), (), s32[]{:S(2)}) async-start(), calls=%async_computation.1 | async-start | bytes 786432 | tf_op jit(solution)/shard_map/psum | solution.py:64
  707.5 2.0 copy-start.5
Sparse Core Ops, SparseCore 0:
  566.3 141.1 all-reduce.3
  713.7 138.3 all-reduce.5
where the time goes:
time: 863 us; the launch traced here: 862 us
  blocking collectives  543 us (63%)
  waiting for transfers between devices  280 us (32%)
  between operations  14.2 us (2%)
  matrix products  12 us (1%)
  other arithmetic  8.78 us (1%)
    pmax x3, blocking collectives, col_lse(): maxima = lax.pmax(jnp.max(scores, axis=0), 'row')  222 us
    psum x3, blocking collectives, col_lse(): totals = lax.psum(jnp.sum(jnp.exp(scores - maxima[None, :]), axis=0), 'row')  188 us
    psum x1, waiting for transfers between devices, shards(): barycentre = lax.psum(partial_value, 'col')  141 us
    psum x1, waiting for transfers between devices, shards(): grad_first, grad_second = lax.psum((first_term, second_term), 'row')  139 us
    pmax x3, blocking collectives, row_lse(): maxima = lax.pmax(jnp.max(scores, axis=1), 'col')  72.8 us
    psum x3, blocking collectives, row_lse(): totals = lax.psum(jnp.sum(jnp.exp(scores - maxima[:, None]), axis=1), 'col')  60.2 us
  transfers between devices with their start and end apart: 2, of which 2 were waited for; matrix products, arithmetic and copies ran while one was open for 0% of the time, Pallas kernels for 0%

commit v1 on v0

--- a/solution.py
+++ b/solution.py
@@ -47,7 +47,20 @@
     ).astype(jnp.bfloat16)
     partial_value = jnp.dot(weights, history, preferred_element_type=jnp.float32)
     scale = 1.0 / math.sqrt(gen_total)
-    barycentre = lax.psum(partial_value, "col")
+
+    def lay_terms(local_x, net_axis):
+        wide_n = lax.axis_size(net_axis)
+        local_out = local_x
+        for to_i in [
+            [(tick, tick ^ hop_no) for tick in range(wide_n)]
+            for hop_no in (1, 2, 4, 8, 16)
+            if hop_no < wide_n
+        ]:
+            y2 = lax.ppermute(local_out, net_axis, to_i)
+            local_out = local_out + y2
+        return local_out
+
+    barycentre = lay_terms(partial_value, "col")
     d_surface = ((surf_f - barycentre) * scale).astype(jnp.bfloat16)
     d_hidden = lax.dot_general(
         d_surface, w_second, (((1,), (1,)), ((), ())), preferred_element_type=jnp.float32

time: 863 us -> 1200 us (1.39)
  waiting for transfers between devices: 280 us -> 601 us
  starting transfers between devices: 0.08 us -> 16.3 us
    ppermute x0 -> x4, waiting for transfers between devices: none -> 450 us  [lay_terms(): y2 = lax.ppermute(local_out, net_axis, to_i)]
    psum x1 -> x0, waiting for transfers between devices: 141 us -> none  [shards(): barycentre = lax.psum(partial_value, 'col')]
    ppermute x0 -> x4, starting transfers between devices: none -> 16.3 us  [lay_terms(): y2 = lax.ppermute(local_out, net_axis, to_i)]
    psum x1, waiting for transfers between devices: 139 us -> 152 us  [shards(): grad_first, grad_second = lax.psum((first_term, second_term), 'row')]
  transfers between devices with their start and end apart: 2 -> 5, of which waited for: 2 -> 5; matrix products, arithmetic and copies ran while one was open for 0% -> 0% of each run, Pallas kernels for 0% -> 0%
where the time goes in v1:
time: 1200 us
  waiting for transfers between devices  601 us (50%)
  blocking collectives  543 us (45%)
  starting transfers between devices  16.3 us (1%)
  between operations  14.2 us (1%)
    ppermute x4, waiting for transfers between devices, lay_terms(): y2 = lax.ppermute(local_out, net_axis, to_i)  450 us
    pmax x3, blocking collectives, col_lse(): maxima = lax.pmax(jnp.max(scores, axis=0), 'row')  222 us
    psum x3, blocking collectives, col_lse(): totals = lax.psum(jnp.sum(jnp.exp(scores - maxima[None, :]), axis=0), 'row')  188 us
    psum x1, waiting for transfers between devices, shards(): grad_first, grad_second = lax.psum((first_term, second_term), 'row')  152 us
    pmax x3, blocking collectives, row_lse(): maxima = lax.pmax(jnp.max(scores, axis=1), 'col')  72.8 us
    psum x3, blocking collectives, row_lse(): totals = lax.psum(jnp.sum(jnp.exp(scores - maxima[:, None]), axis=1), 'col')  60.2 us
  transfers between devices with their start and end apart: 5, of which 5 were waited for; matrix products, arithmetic and copies ran while one was open for 0% of the time, Pallas kernels for 0%

profile of v1, /device:TPU:1, one launch (start us, length us, event | category | flops | bytes accessed | tf_op | source)
XLA Modules:
  0.0 1202.3 jit_solution(4471996700964385678)
XLA Ops:
  7.2 0.0 all-reduce.3.cloned.1.call-start
  7.2 2.2 multiply_reduce_fusion
  9.4 1.3 multiply_convert_fusion.2
  10.8 0.8 fusion
  11.6 1.0 copy-done.1
  12.5 1.5 fusion.3
  14.1 68.9 %pmax.42 = f32[1024]{0:T(1024)S(1)} all-reduce(f32[1024]{0:T(1024)S(1)} %get-tuple-element.10), channel_id=1, replica_groups=mesh['row'=32,'col'=16] {'row'}, use_global_device_ids=true, to_apply=%region_3.4 | all-reduce | flops 1024 | bytes 8192 | tf_op jit(solution)/shard_map/pmax | solution.py:18
  83.0 0.4 exponential_reduce_fusion.5
  83.4 62.7 %psum.56 = f32[1024]{0:T(1024)S(1)} all-reduce(f32[1024]{0:T(1024)S(1)} %exponential_reduce_fusion.5), channel_id=1, replica_groups=mesh['row'=32,'col'=16] {'row'}, use_global_device_ids=true, to_apply=%region_5.6 | all-reduce | flops 1024 | bytes 8192 | tf_op jit(solution)/shard_map/psum | solution.py:19
  146.1 0.3 fusion.4
  146.4 28.8 %pmax.43 = f32[512]{0:T(512)S(1)} all-reduce(f32[512]{0:T(512)S(1)} %fusion.4), channel_id=1, replica_groups=mesh['row'=32,'col'=16] {'col'}, use_global_device_ids=true, to_apply=%region_7.8 | all-reduce | flops 512 | bytes 4096 | tf_op jit(solution)/shard_map/pmax | solution.py:12
  175.2 0.6 exponential_reduce_fusion.4
  175.7 20.1 %psum.57 = f32[512]{0:T(512)S(1)} all-reduce(f32[512]{0:T(512)S(1)} %exponential_reduce_fusion.4), channel_id=1, replica_groups=mesh['row'=32,'col'=16] {'col'}, use_global_device_ids=true, to_apply=%region_9.10 | all-reduce | flops 512 | bytes 4096 | tf_op jit(solution)/shard_map/psum | solution.py:13
  195.8 0.3 fusion.5
  196.1 76.7 %pmax.44 = f32[1024]{0:T(1024)S(1)} all-reduce(f32[1024]{0:T(1024)S(1)} %fusion.5), channel_id=1, replica_groups=mesh['row'=32,'col'=16] {'row'}, use_global_device_ids=true, to_apply=%region_11.12 | all-reduce | flops 1024 | bytes 8192 | tf_op jit(solution)/shard_map/pmax | solution.py:18
  272.8 0.5 exponential_reduce_fusion.3
  273.3 62.7 %psum.58 = f32[1024]{0:T(1024)S(1)} all-reduce(f32[1024]{0:T(1024)S(1)} %exponential_reduce_fusion.3), channel_id=1, replica_groups=mesh['row'=32,'col'=16] {'row'}, use_global_device_ids=true, to_apply=%region_13.14 | all-reduce | flops 1024 | bytes 8192 | tf_op jit(solution)/shard_map/psum | solution.py:19
  336.0 0.3 fusion.6
  336.2 22.0 %pmax.45 = f32[512]{0:T(512)S(1)} all-reduce(f32[512]{0:T(512)S(1)} %fusion.6), channel_id=1, replica_groups=mesh['row'=32,'col'=16] {'col'}, use_global_device_ids=true, to_apply=%region_15.16 | all-reduce | flops 512 | bytes 4096 | tf_op jit(solution)/shard_map/pmax | solution.py:12
  358.3 0.6 exponential_reduce_fusion.2
  358.8 20.1 %psum.59 = f32[512]{0:T(512)S(1)} all-reduce(f32[512]{0:T(512)S(1)} %exponential_reduce_fusion.2), channel_id=1, replica_groups=mesh['row'=32,'col'=16] {'col'}, use_global_device_ids=true, to_apply=%region_17.18 | all-reduce | flops 512 | bytes 4096 | tf_op jit(solution)/shard_map/psum | solution.py:13
  378.9 0.3 fusion.7
  379.2 76.7 %pmax.46 = f32[1024]{0:T(1024)S(1)} all-reduce(f32[1024]{0:T(1024)S(1)} %fusion.7), channel_id=1, replica_groups=mesh['row'=32,'col'=16] {'row'}, use_global_device_ids=true, to_apply=%region_19.20 | all-reduce | flops 1024 | bytes 8192 | tf_op jit(solution)/shard_map/pmax | solution.py:18
  455.8 0.5 exponential_reduce_fusion.1
  456.3 62.7 %psum.60 = f32[1024]{0:T(1024)S(1)} all-reduce(f32[1024]{0:T(1024)S(1)} %exponential_reduce_fusion.1), channel_id=1, replica_groups=mesh['row'=32,'col'=16] {'row'}, use_global_device_ids=true, to_apply=%region_21.22 | all-reduce | flops 1024 | bytes 8192 | tf_op jit(solution)/shard_map/psum | solution.py:19
  519.0 0.3 fusion.8
  519.3 22.0 %pmax.47 = f32[512]{0:T(512)S(1)} all-reduce(f32[512]{0:T(512)S(1)} %fusion.8), channel_id=1, replica_groups=mesh['row'=32,'col'=16] {'col'}, use_global_device_ids=true, to_apply=%region_23.24 | all-reduce | flops 512 | bytes 4096 | tf_op jit(solution)/shard_map/pmax | solution.py:12
  541.3 0.6 exponential_reduce_fusion
  541.9 20.1 %psum.61 = f32[512]{0:T(512)S(1)} all-reduce(f32[512]{0:T(512)S(1)} %exponential_reduce_fusion), channel_id=1, replica_groups=mesh['row'=32,'col'=16] {'col'}, use_global_device_ids=true, to_apply=%region_25.26 | all-reduce | flops 512 | bytes 4096 | tf_op jit(solution)/shard_map/psum | solution.py:13
  562.0 2.9 fusion.13
  564.9 3.4 collective-permute-start
  568.2 31.0 %collective-permute-done = f32[512,1024]{1,0:T(8,128)S(1)} collective-permute-done((f32[512,1024]{1,0:T(8,128)S(1)}, f32[512,1024]{1,0:T(8,128)S(1)}, u32[]{:S(2)}, u32[]{:S(2)}) %collective-permute-start) | collective-permute-done | bytes 2097184 | tf_op jit(solution)/shard_map/ppermute | solution.py:59
  599.3 0.6 add.117
  599.8 1.9 collective-permute-start.1
  601.7 84.5 %collective-permute-done.1 = f32[512,1024]{1,0:T(8,128)S(1)} collective-permute-done((f32[512,1024]{1,0:T(8,128)S(1)}, f32[512,1024]{1,0:T(8,128)S(1)}, u32[]{:S(2)}, u32[]{:S(2)}) %collective-permute-start.1) | collective-permute-done | bytes 2097184 | tf_op jit(solution)/shard_map/ppermute | solution.py:59
  686.2 0.6 add.118
  686.8 3.0 collective-permute-start.2
  689.8 225.3 %collective-permute-done.2 = f32[512,1024]{1,0:T(8,128)S(1)} collective-permute-done((f32[512,1024]{1,0:T(8,128)S(1)}, f32[512,1024]{1,0:T(8,128)S(1)}, u32[]{:S(2)}, u32[]{:S(2)}) %collective-permute-start.2) | collective-permute-done | bytes 2097184 | tf_op jit(solution)/shard_map/ppermute | solution.py:59
  915.1 0.4 add.119
  915.5 8.0 collective-permute-start.3
  923.6 109.0 %collective-permute-done.3 = f32[512,1024]{1,0:T(8,128)} collective-permute-done((f32[512,1024]{1,0:T(8,128)S(1)}, f32[512,1024]{1,0:T(8,128)}, u32[]{:S(2)}, u32[]{:S(2)}) %collective-permute-start.3) | collective-permute-done | bytes 2097184 | tf_op jit(solution)/shard_map/ppermute | solution.py:59
  1032.6 2.5 fusion.2
  1035.1 1.0 copy-done.2
  1036.1 1.0 fusion.22
  1037.0 3.4 fusion.12
  1040.5 151.6 %all-reduce.3.cloned.1.call-done = (f32[128,512]{0,1:T(8,128)}, f32[512,64]{0,1:T(8,128)}) async-done(((f32[128,512]{0,1:T(8,128)}, f32[512,64]{0,1:T(8,128)}), (f32[128,512]{0,1:T(8,128)}, f32[512,64]{0,1:T(8,128)})) %all-reduce.3.cloned.1.call-update) | async-done | bytes 393232 | tf_op jit(solution)/shard_map/psum | solution.py:77
  1192.1 1.8 copy.6
  1193.9 1.6 copy.9
  (21 shorter events, 0.1 us)
Async XLA Ops:
  7.2 3.6 copy-start
  7.2 2.2 copy-start.7
  7.2 2.2 copy-start.6
  7.2 1184.9 %all-reduce.3.cloned.1.call-start = ((), (), s32[]{:S(2)}) async-start(), calls=%async_computation | async-start | bytes 786432 | tf_op jit(solution)/shard_map/psum | solution.py:77
  10.8 0.8 copy-start.4
  10.8 1.8 copy-start.1
  11.6 2.5 copy-start.3
  564.9 34.4 %collective-permute-start = (f32[512,1024]{1,0:T(8,128)S(1)}, f32[512,1024]{1,0:T(8,128)S(1)}, u32[]{:S(2)}, u32[]{:S(2)}) collective-permute-start(f32[512,1024]{1,0:T(8,128)S(1)} %fusion.13), channel_id=1, source_target_pairs={{0,1},{1,0},{2,3},{3,2},{4,5},{5,4},{6,7},{7,6},{8,9},{9,8},{10,11... | collective-permute-start | bytes 6291464 | tf_op jit(solution)/shard_map/ppermute | solution.py:59
  599.8 86.4 %collective-permute-start.1 = (f32[512,1024]{1,0:T(8,128)S(1)}, f32[512,1024]{1,0:T(8,128)S(1)}, u32[]{:S(2)}, u32[]{:S(2)}) collective-permute-start(f32[512,1024]{1,0:T(8,128)S(1)} %add.117), channel_id=1, source_target_pairs={{0,2},{1,3},{2,0},{3,1},{4,6},{5,7},{6,4},{7,5},{8,10},{9,11},{10,... | collective-permute-start | bytes 6291464 | tf_op jit(solution)/shard_map/ppermute | solution.py:59
  686.8 228.3 %collective-permute-start.2 = (f32[512,1024]{1,0:T(8,128)S(1)}, f32[512,1024]{1,0:T(8,128)S(1)}, u32[]{:S(2)}, u32[]{:S(2)}) collective-permute-start(f32[512,1024]{1,0:T(8,128)S(1)} %add.118), channel_id=1, source_target_pairs={{0,4},{1,5},{2,6},{3,7},{4,0},{5,1},{6,2},{7,3},{8,12},{9,13},{10,... | collective-permute-start | bytes 6291464 | tf_op jit(solution)/shard_map/ppermute | solution.py:59
  915.5 117.0 %collective-permute-start.3 = (f32[512,1024]{1,0:T(8,128)S(1)}, f32[512,1024]{1,0:T(8,128)}, u32[]{:S(2)}, u32[]{:S(2)}) collective-permute-start(f32[512,1024]{1,0:T(8,128)S(1)} %add.119), channel_id=1, source_target_pairs={{0,8},{1,9},{2,10},{3,11},{4,12},{5,13},{6,14},{7,15},{8,0},{9,1},... | collective-permute-start | bytes 6291464 | tf_op jit(solution)/shard_map/ppermute | solution.py:59
  923.5 112.5 %copy-start.5 = (bf16[512,512]{1,0:T(8,128)(2,1)S(1)}, bf16[512,512]{1,0:T(8,128)(2,1)}, u32[]{:S(2)}) copy-start(bf16[512,512]{1,0:T(8,128)(2,1)} %copy-done.4) | copy-start | bytes 1572868
  1035.1 1.0 copy-start.2
Sparse Core Ops, SparseCore 0:
  1040.6 151.4 all-reduce.2
